TPU v7x, 32 devices: a whole 2x2x4 slice. The times are simulated.
32 devices in a mesh: patch: 16 (over z, y, core), band: 2 (over x).
Axes of the slice: x: 2, y: 2, z: 4, core: 2. Of those that a mesh axis runs over, the one named last changes fastest.
Arguments:
- latents: float32 [10240, 512], P('patch', 'band'), may hold values from -6 to 6
- edge_latents: float32 [81920, 512], P(('patch', 'band')), may hold values from -6 to 6
- edge_sender: int32 [81920], P(('patch', 'band')), may hold values from 0 to 575, as said below
- edge_receiver: int32 [81920], P(('patch', 'band')), may hold values from 0 to 319
- block_counts: int32 [640], P(('patch', 'band')), may hold values from 16 to 128, as said below
- send_rows: int32 [32, 32, 8], P(('patch', 'band')), may hold values from 0 to 319
- edge_first_weight: bfloat16 [2, 1536, 512], replicated, may hold values from -0.15625 to 0.15625
- edge_first_bias: float32 [2, 512], replicated, may hold values from -3 to 3
- edge_second_weight: bfloat16 [2, 512, 512], replicated
- edge_gain: float32 [2, 512], replicated, may hold values from 0.1 to 1.9
- edge_offset: float32 [2, 512], replicated, may hold values from -3 to 3
- node_first_weight: bfloat16 [2, 1024, 512], replicated, may hold values from -0.1875 to 0.1875
- node_first_bias: float32 [2, 512], replicated, may hold values from -3 to 3
- node_second_weight: bfloat16 [2, 512, 512], replicated
- node_gain: float32 [2, 512], replicated, may hold values from 0.1 to 1.9
- node_offset: float32 [2, 512], replicated, may hold values from -3 to 3
Outputs:
- new_nodes: float32 [10240, 512], P(('patch', 'band'))
- new_edges: float32 [81920, 512], P(('patch', 'band'))
Inputs may be any that keep to these rules, and one draw needn't show every extreme that they name: `edge_sender`: an entry below 320 names a node row of the edge's own device; an entry k above names slot (k - 320) % 8 of the rows that device (k - 320) // 8 sends to the edge's device. `block_counts`: the used slots of a block are its first ones; every device has a full block. send_rows[d, q] lists node rows of device d, numbered within d, that device q receives from d.
All inputs are finite; a program needn't handle non-finite values.
Results may differ from a plain program's by a relative error of at most 0.0045.
Values may be sent and summed in bfloat16 or wider, within the bound.
A program may use at most 128 MiB of HBM per device.

v0:
```python
import jax
import jax.numpy as jnp
from jax import lax
from jax.sharding import PartitionSpec as P

epsilon = 1e-05


def layer_norm(values, norm_gain, norm_offset):
    centre = values - jnp.mean(values, axis=-1, keepdims=True)
    spread = jnp.mean(centre * centre, axis=-1, keepdims=True)
    return centre * lax.rsqrt(spread + epsilon) * norm_gain + norm_offset


def perceptron(pieces, first_weight, first_bias, second_weight, norm_gain, norm_offset):
    columns = pieces[0].shape[1]
    running = first_bias
    for position in range(len(pieces)):
        running = running + jnp.dot(
            pieces[position],
            first_weight[position * columns : (position + 1) * columns],
            preferred_element_type=jnp.float32,
        )
    active = (running * jax.nn.sigmoid(running)).astype(jnp.bfloat16)
    result = jnp.dot(active, second_weight, preferred_element_type=jnp.float32)
    return layer_norm(result, norm_gain, norm_offset)


def fetch_halo(node_low, send_lists):
    outgoing = node_low[send_lists]
    return lax.all_to_all(outgoing, ("patch", "band"), split_axis=0, concat_axis=0, tiled=True)


def shards(
    latents,
    edge_latents,
    edge_sender,
    edge_receiver,
    block_counts,
    send_rows,
    edge_first_weight,
    edge_first_bias,
    edge_second_weight,
    edge_gain,
    edge_offset,
    node_first_weight,
    node_first_bias,
    node_second_weight,
    node_gain,
    node_offset,
):
    layers = edge_first_weight.shape[0]
    send_lists = send_rows[0]
    block_length = edge_sender.shape[0] // block_counts.shape[0]
    usable = (jnp.arange(block_length, dtype=jnp.int32)[None, :] < block_counts[:, None]).reshape(
        -1
    )
    first_rows = None
    node_state = lax.all_to_all(latents, "band", split_axis=0, concat_axis=1, tiled=True)
    edge_state = edge_latents
    node_count = node_state.shape[0]
    matches = jnp.arange(node_count, dtype=jnp.int32)[:, None] == edge_receiver[None, :]
    receiver_hot = matches.astype(jnp.bfloat16)
    summing_hot = (matches & usable[None, :]).astype(jnp.bfloat16)
    for layer_index in range(layers):
        node_low = node_state.astype(jnp.bfloat16)
        incoming = fetch_halo(node_low, send_lists)
        sender_table = jnp.concatenate([node_low, incoming.reshape(-1, node_low.shape[1])], axis=0)
        receiver_rows = lax.dot_general(
            receiver_hot, node_low, (((0,), (0,)), ((), ())), preferred_element_type=jnp.float32
        ).astype(jnp.bfloat16)
        edge_low = edge_state.astype(jnp.bfloat16)
        update = perceptron(
            (edge_low, sender_table[edge_sender], receiver_rows),
            edge_first_weight[layer_index],
            edge_first_bias[layer_index],
            edge_second_weight[layer_index],
            edge_gain[layer_index],
            edge_offset[layer_index],
        )
        edge_state = edge_state + jnp.where(usable[:, None], update, jnp.zeros_like(update))
        edge_out_low = edge_state.astype(jnp.bfloat16)
        summed = jnp.dot(summing_hot, edge_out_low, preferred_element_type=jnp.float32)
        summed_low = summed.astype(jnp.bfloat16)
        node_state = node_state + perceptron(
            (node_low, summed_low),
            node_first_weight[layer_index],
            node_first_bias[layer_index],
            node_second_weight[layer_index],
            node_gain[layer_index],
            node_offset[layer_index],
        )
    return (node_state, edge_state)


def solution(mesh):
    return jax.shard_map(
        shards,
        mesh=mesh,
        in_specs=(
            P("patch", "band"),
            P(("patch", "band"), None),
            P(("patch", "band")),
            P(("patch", "band")),
            P(("patch", "band")),
            P(("patch", "band"), None, None),
            P(),
            P(),
            P(),
            P(),
            P(),
            P(),
            P(),
            P(),
            P(),
            P(),
        ),
        out_specs=(P(("patch", "band"), None), P(("patch", "band"), None)),
        check_vma=False,
    )
```

profile of v0, /device:TPU:0, one launch (start us, length us, event | category | flops | bytes accessed | tf_op | source)
XLA Modules:
  0.0 148.7 jit_solution(3055805901451270836)
XLA Ops:
  0.6 4.2 %all-to-all-start = ((f32[2,320,256]{2,1,0:T(8,128)}), f32[2,320,256]{2,1,0:T(8,128)S(1)}, u32[]{:S(2)}, u32[]{:S(2)}) async-start(f32[2,320,256]{2,1,0:T(8,128)} %bitcast.105), calls=%async_computation | async-start | bytes 1310720 | tf_op jit(solution)/shard_map/all_to_all | solution.py:59
  6.5 1.4 fusion.90
  7.8 5.9 %copy.32 = f32[2560,512]{0,1:T(8,128)} copy(f32[2560,512]{1,0:T(8,128)} %param.17) | data formatting | bytes 10485760 | tf_op args[1]
  13.7 6.5 %fusion.6 = f32[2560,512]{1,0:T(8,128)} fusion(f32[2560,512]{1,0:T(8,128)} %param.17, bf16[2,1536,512]{2,1,0:T(8,128)(2,1)} %param.22), kind=kOutput, calls=%fused_computation.17 | convolution fusion | flops 1343488000 | bytes 11010048 | tf_op jit(solution)/shard_map/dot_general | solution.py:19
  24.0 0.8 copy-done.2
  24.9 1.9 %gather_fusion = bf16[256,512]{1,0:T(8,128)(2,1)} fusion(bf16[320,512]{1,0:T(8,128)(2,1)S(1)} %convert_element_type.50, s32[1024]{0:T(1024)S(1)} %pad_clamp_fusion.1), kind=kCustom, calls=%fused_computation | custom fusion | bytes 525312 | tf_op jit(solution)/shard_map/gather | solution.py:30
  26.7 7.1 %all-to-all-start.1 = ((bf16[32,8,512]{2,1,0:T(8,128)(2,1)}), bf16[32,8,512]{2,1,0:T(8,128)(2,1)S(1)}, u32[]{:S(2)}, u32[]{:S(2)}) async-start(bf16[32,8,512]{2,1,0:T(8,128)(2,1)} %bitcast.8), calls=%async_computation.1 | async-start | bytes 524288 | tf_op jit(solution)/shard_map/all_to_all | solution.py:31
  33.9 2.2 %convolution_add_fusion.3 = f32[320,512]{1,0:T(8,128)} fusion(bf16[320,512]{1,0:T(8,128)(2,1)S(1)} %bitcast.102, bf16[2,1024,512]{2,1,0:T(8,128)(2,1)} %param.27, f32[512]{0:T(512)S(1)} %bitcast.113), kind=kOutput, calls=%fused_computation.33 | convolution fusion | flops 167936000 | bytes 1509376 | tf_op jit(solution)/shard_map/dot_general | solution.py:19
  36.2 3.1 %convolution_convert_fusion.1 = bf16[2560,512]{1,0:T(8,128)(2,1)} fusion(bf16[320,512]{1,0:T(8,128)(2,1)S(1)} %convert_element_type.50, s32[2560]{0:T(1024)S(1)} %copy-done.36), kind=kOutput, calls=%fused_computation.11 | convolution fusion | flops 840990720 | bytes 2959360 | tf_op jit(solution)/shard_map/dot_general | solution.py:69
  39.2 5.3 %all-to-all-done.1 = bf16[32,8,512]{2,1,0:T(8,128)(2,1)S(1)} async-done(((bf16[32,8,512]{2,1,0:T(8,128)(2,1)}), bf16[32,8,512]{2,1,0:T(8,128)(2,1)S(1)}, u32[]{:S(2)}, u32[]{:S(2)}) %all-to-all-start.1) | async-done | bytes 262176 | tf_op jit(solution)/shard_map/all_to_all | solution.py:31
  44.6 7.8 %gather_fusion.1 = bf16[2560,512]{1,0:T(8,128)(2,1)S(1)} fusion(bf16[576,512]{1,0:T(8,128)(2,1)S(1)} %pad_maximum_fusion, s32[3072]{0:T(1024)S(1)} %pad_clamp_fusion), kind=kCustom, calls=%fused_computation.1 | custom fusion | bytes 5253120 | tf_op jit(solution)/shard_map/gather | solution.py:74
  52.4 4.9 %fusion.61 = f32[2560,512]{1,0:T(8,128)} fusion(bf16[2560,512]{1,0:T(8,128)(2,1)S(1)} %gather_fusion.1, bf16[2,1536,512]{2,1,0:T(8,128)(2,1)} %param.22), kind=kOutput, calls=%fused_computation.59 | convolution fusion | flops 1342177280 | bytes 8388608 | tf_op jit(solution)/shard_map/dot_general | solution.py:19
  57.4 11.1 %fusion.92 = (f32[2560]{0:T(1024)S(1)}, f32[2560,512]{0,1:T(8,128)}) fusion(bf16[2,512,512]{2,1,0:T(8,128)(2,1)} %param.24, f32[2560,512]{1,0:T(8,128)} %fusion.61, f32[2560,512]{1,0:T(8,128)} %fusion.6, bf16[2560,512]{1,0:T(8,128)(2,1)} %convolution_convert_fusion.1, f32[512]{0:T(512)S(1)} %bitcast.119, bf16[2,1536,512]{2,1,0:T(8,128)(2,1)} %param.22), kind=kOutput, calls=%fused_computation.101 | convolution fusion | flops 2696148480 | bytes 19410944 | tf_op jit(solution)/shard_map/dot_general | solution.py:25
  68.4 3.2 %multiply_reduce_fusion.1 = f32[2560]{0:T(1024)S(1)} fusion(f32[2560,512]{0,1:T(8,128)} %get-tuple-element.23, f32[2560]{0:T(1024)S(1)} %broadcast_multiply_fusion.1), kind=kLoop, calls=%fused_computation.8 | loop fusion | flops 3929600 | bytes 5263360 | tf_op jit(solution)/shard_map/reduce_sum | solution.py:11
  71.7 0.8 copy-done.1
  72.5 6.3 %select_add_fusion.1 = f32[2560,512]{0,1:T(8,128)} fusion(f32[2560,512]{0,1:T(8,128)} %copy.32, f32[2560,512]{0,1:T(8,128)S(1)} %copy-done.1, f32[512]{0:T(512)S(1)} %bitcast.117, f32[512]{0:T(512)S(1)} %bitcast.116, f32[2560]{0:T(1024)S(1)} %add_rsqrt_fusion.1, f32[2560]{0:T(1024)S(1)} %broadcast_multiply_fusion.1, pred[2560]{0:T(1024)(128)(4,1)S(1)} %copy-done.13), kind=kLoop, calls=%fused_computation.7 | loop fusion | flops 7864320 | bytes 15755776 | tf_op jit(solution)/shard_map/add | solution.py:81
  78.8 4.1 %multiply_convert_fusion.3 = bf16[320,512]{1,0:T(8,128)(2,1)S(1)} fusion(f32[320,512]{1,0:T(8,128)S(1)} %copy-done.10, f32[2560,512]{0,1:T(8,128)} %select_add_fusion.1, s32[2560]{0:T(1024)S(1)} %copy-done.37, pred[2560]{0:T(1024)(128)(4,1)S(1)} %copy-done.13, bf16[2,1024,512]{2,1,0:T(8,128)(2,1)} %param.27), kind=kOutput, calls=%fused_computation.42 | convolution fusion | flops 1010728960 | bytes 6763008 | tf_op jit(solution)/shard_map/dot_general | solution.py:19
  84.4 1.9 %gather_fusion.2 = bf16[256,512]{1,0:T(8,128)(2,1)} fusion(bf16[320,512]{1,0:T(8,128)(2,1)S(1)} %fusion.85, s32[1024]{0:T(1024)S(1)} %pad_clamp_fusion.1), kind=kCustom, calls=%fused_computation.2 | custom fusion | bytes 525312 | tf_op jit(solution)/shard_map/gather | solution.py:30
  86.3 3.1 %convolution_convert_fusion = bf16[2560,512]{1,0:T(8,128)(2,1)} fusion(bf16[320,512]{1,0:T(8,128)(2,1)S(1)} %fusion.85, s32[2560]{0:T(1024)S(1)} %copy-done.37), kind=kOutput, calls=%fused_computation.10 | convolution fusion | flops 840990720 | bytes 2959360 | tf_op jit(solution)/shard_map/dot_general | solution.py:69
  89.4 2.8 %all-to-all-start.2 = ((bf16[32,8,512]{2,1,0:T(8,128)(2,1)}), bf16[32,8,512]{2,1,0:T(8,128)(2,1)S(1)}, u32[]{:S(2)}, u32[]{:S(2)}) async-start(bf16[32,8,512]{2,1,0:T(8,128)(2,1)} %bitcast.23), calls=%async_computation.2 | async-start | bytes 524288 | tf_op jit(solution)/shard_map/all_to_all | solution.py:31
  92.2 2.2 %convolution_add_fusion.1 = f32[320,512]{1,0:T(8,128)} fusion(bf16[320,512]{1,0:T(8,128)(2,1)S(1)} %fusion.85, bf16[2,1024,512]{2,1,0:T(8,128)(2,1)} %param.27, f32[512]{0:T(512)S(1)} %bitcast.112), kind=kOutput, calls=%fused_computation.31 | convolution fusion | flops 167936000 | bytes 1509376 | tf_op jit(solution)/shard_map/dot_general | solution.py:19
  94.4 6.5 %fusion.16 = f32[2560,512]{1,0:T(8,128)} fusion(f32[2560,512]{0,1:T(8,128)} %select_add_fusion.1, bf16[2,1536,512]{2,1,0:T(8,128)(2,1)} %param.22), kind=kOutput, calls=%fused_computation.27 | convolution fusion | flops 1343488000 | bytes 11010048 | tf_op jit(solution)/shard_map/dot_general | solution.py:19
  100.9 1.7 %all-to-all-done.2 = bf16[32,8,512]{2,1,0:T(8,128)(2,1)S(1)} async-done(((bf16[32,8,512]{2,1,0:T(8,128)(2,1)}), bf16[32,8,512]{2,1,0:T(8,128)(2,1)S(1)}, u32[]{:S(2)}, u32[]{:S(2)}) %all-to-all-start.2) | async-done | bytes 262176 | tf_op jit(solution)/shard_map/all_to_all | solution.py:31
  102.7 7.7 %gather_fusion.3 = bf16[2560,512]{1,0:T(8,128)(2,1)S(1)} fusion(bf16[576,512]{1,0:T(8,128)(2,1)S(1)} %pad_maximum_fusion.1, s32[3072]{0:T(1024)S(1)} %pad_clamp_fusion), kind=kCustom, calls=%fused_computation.3 | custom fusion | bytes 5253120 | tf_op jit(solution)/shard_map/gather | solution.py:74
  110.4 4.9 %fusion.51 = f32[2560,512]{1,0:T(8,128)} fusion(bf16[2560,512]{1,0:T(8,128)(2,1)S(1)} %gather_fusion.3, bf16[2,1536,512]{2,1,0:T(8,128)(2,1)} %param.22), kind=kOutput, calls=%fused_computation.50 | convolution fusion | flops 1342177280 | bytes 8388608 | tf_op jit(solution)/shard_map/dot_general | solution.py:19
  115.3 11.1 %fusion.96 = (f32[2560]{0:T(1024)S(1)}, f32[2560,512]{0,1:T(8,128)}) fusion(bf16[2,512,512]{2,1,0:T(8,128)(2,1)} %param.24, f32[2560,512]{1,0:T(8,128)} %fusion.51, f32[2560,512]{1,0:T(8,128)} %fusion.16, bf16[2560,512]{1,0:T(8,128)(2,1)} %convolution_convert_fusion, f32[512]{0:T(512)S(1)} %bitcast.118, bf16[2,1536,512]{2,1,0:T(8,128)(2,1)} %param.22), kind=kOutput, calls=%fused_computation.103 | convolution fusion | flops 2696148480 | bytes 19410944 | tf_op jit(solution)/shard_map/dot_general | solution.py:25
  126.4 3.2 %multiply_reduce_fusion = f32[2560]{0:T(1024)S(1)} fusion(f32[2560,512]{0,1:T(8,128)} %get-tuple-element.27, f32[2560]{0:T(1024)S(1)} %broadcast_multiply_fusion), kind=kLoop, calls=%fused_computation.5 | loop fusion | flops 3929600 | bytes 5263360 | tf_op jit(solution)/shard_map/reduce_sum | solution.py:11
  129.6 0.8 copy-done
  130.4 6.2 %select_add_fusion = f32[2560,512]{0,1:T(8,128)} fusion(f32[2560,512]{0,1:T(8,128)} %select_add_fusion.1, f32[2560,512]{0,1:T(8,128)S(1)} %copy-done, f32[512]{0:T(512)S(1)} %bitcast.115, f32[512]{0:T(512)S(1)} %bitcast.114, f32[2560]{0:T(1024)S(1)} %add_rsqrt_fusion, f32[2560]{0:T(1024)S(1)} %broadcast_multiply_fusion, pred[2560]{0:T(1024)(128)(4,1)S(1)} %copy-done.14), kind=kLoop, calls=%fused_computation.4 | loop fusion | flops 7864320 | bytes 15755776 | tf_op jit(solution)/shard_map/add | solution.py:81
  136.6 5.9 %copy.33 = f32[2560,512]{1,0:T(8,128)} copy(f32[2560,512]{0,1:T(8,128)} %select_add_fusion) | data formatting | bytes 10485760
  142.7 4.1 %multiply_convert_fusion.2 = bf16[320,512]{1,0:T(8,128)(2,1)S(1)} fusion(f32[320,512]{1,0:T(8,128)S(1)} %copy-done.9, f32[2560,512]{0,1:T(8,128)} %select_add_fusion, s32[2560]{0:T(1024)S(1)} %copy-done.38, pred[2560]{0:T(1024)(128)(4,1)S(1)} %copy-done.14, bf16[2,1024,512]{2,1,0:T(8,128)(2,1)} %param.27), kind=kOutput, calls=%fused_computation.39 | convolution fusion | flops 1010728960 | bytes 6763008 | tf_op jit(solution)/shard_map/dot_general | solution.py:19
  147.6 1.1 add_add_fusion
  (107 shorter events, 7.8 us)
Async XLA Ops:
  0.6 23.3 %all-to-all-start = ((f32[2,320,256]{2,1,0:T(8,128)}), f32[2,320,256]{2,1,0:T(8,128)S(1)}, u32[]{:S(2)}, u32[]{:S(2)}) async-start(f32[2,320,256]{2,1,0:T(8,128)} %bitcast.105), calls=%async_computation | async-start | bytes 1310720 | tf_op jit(solution)/shard_map/all_to_all | solution.py:59
  13.7 6.5 %copy-start.35 = (s32[20]{0:T(128)S(1)}, s32[20]{0:T(128)}, u32[]{:S(2)}) copy-start(s32[20]{0:T(128)} %param.20) | copy-start | bytes 244
  13.7 7.2 %copy-start.28 = (f32[2,512]{1,0:T(2,128)S(1)}, f32[2,512]{1,0:T(2,128)}, u32[]{:S(2)}) copy-start(f32[2,512]{1,0:T(2,128)} %param.25) | copy-start | bytes 12292
  13.7 7.8 %copy-start.29 = (f32[2,512]{1,0:T(2,128)S(1)}, f32[2,512]{1,0:T(2,128)}, u32[]{:S(2)}) copy-start(f32[2,512]{1,0:T(2,128)} %param.26) | copy-start | bytes 12292
  13.7 8.4 %copy-start.30 = (f32[2,512]{1,0:T(2,128)S(1)}, f32[2,512]{1,0:T(2,128)}, u32[]{:S(2)}) copy-start(f32[2,512]{1,0:T(2,128)} %param.28) | copy-start | bytes 12292
  13.7 9.0 %copy-start.31 = (f32[2,512]{1,0:T(2,128)S(1)}, f32[2,512]{1,0:T(2,128)}, u32[]{:S(2)}) copy-start(f32[2,512]{1,0:T(2,128)} %param.30) | copy-start | bytes 12292
  13.7 9.6 %copy-start.32 = (f32[2,512]{1,0:T(2,128)S(1)}, f32[2,512]{1,0:T(2,128)}, u32[]{:S(2)}) copy-start(f32[2,512]{1,0:T(2,128)} %param.31) | copy-start | bytes 12292
  20.2 15.9 %copy-start.36 = (s32[2560]{0:T(1024)S(1)}, s32[2560]{0:T(1024)}, u32[]{:S(2)}) copy-start(s32[2560]{0:T(1024)} %param.19) | copy-start | bytes 30724
  26.7 17.8 %all-to-all-start.1 = ((bf16[32,8,512]{2,1,0:T(8,128)(2,1)}), bf16[32,8,512]{2,1,0:T(8,128)(2,1)S(1)}, u32[]{:S(2)}, u32[]{:S(2)}) async-start(bf16[32,8,512]{2,1,0:T(8,128)(2,1)} %bitcast.8), calls=%async_computation.1 | async-start | bytes 524288 | tf_op jit(solution)/shard_map/all_to_all | solution.py:31
  52.4 5.0 %copy-start.34 = (f32[1,512]{1,0:T(1,128)S(1)}, f32[1,512]{1,0:T(1,128)}, u32[]{:S(2)}) copy-start(f32[1,512]{1,0:T(1,128)} %get-tuple-element.19) | copy-start | bytes 6148
  72.5 6.3 %copy-start.10 = (f32[320,512]{1,0:T(8,128)S(1)}, f32[320,512]{1,0:T(8,128)}, u32[]{:S(2)}) copy-start(f32[320,512]{1,0:T(8,128)} %convolution_add_fusion.3) | copy-start | bytes 1966084
  72.5 6.3 %copy-start.37 = (s32[2560]{0:T(1024)S(1)}, s32[2560]{0:T(1024)}, u32[]{:S(2)}) copy-start(s32[2560]{0:T(1024)} %param.19) | copy-start | bytes 30724
  78.8 4.1 %copy-start.7 = (bf16[2,512,512]{2,1,0:T(8,128)(2,1)S(1)}, bf16[2,512,512]{2,1,0:T(8,128)(2,1)}, u32[]{:S(2)}) copy-start(bf16[2,512,512]{2,1,0:T(8,128)(2,1)} %param.29) | copy-start | bytes 3145732
  78.8 5.4 %copy-start.3 = (f32[2,40,8,256]{3,2,0,1:T(8,128)S(1)}, f32[2,40,8,256]{3,2,0,1:T(8,128)}, u32[]{:S(2)}) copy-start(f32[2,40,8,256]{3,2,0,1:T(8,128)} %copy-done.2) | copy-start | bytes 1966084
  78.8 5.4 %copy-start.17 = (f32[1,512]{1,0:T(1,128)S(1)}, f32[1,512]{1,0:T(1,128)}, u32[]{:S(2)}) copy-start(f32[1,512]{1,0:T(1,128)} %get-tuple-element.11) | copy-start | bytes 6148
  78.8 5.4 %copy-start.19 = (f32[1,512]{1,0:T(1,128)S(1)}, f32[1,512]{1,0:T(1,128)}, u32[]{:S(2)}) copy-start(f32[1,512]{1,0:T(1,128)} %get-tuple-element.13) | copy-start | bytes 6148
  83.4 6.0 %copy-start.11 = (f32[320]{0:T(512)}, f32[320]{0:T(512)S(1)}, u32[]{:S(2)}) copy-start(f32[320]{0:T(512)S(1)} %broadcast_multiply_fusion.3) | copy-start | bytes 3844
  83.7 5.7 %copy-start.15 = (f32[320]{0:T(512)}, f32[320]{0:T(512)S(1)}, u32[]{:S(2)}) copy-start(f32[320]{0:T(512)S(1)} %add_rsqrt_fusion.3) | copy-start | bytes 3844
  86.3 5.9 %copy-start.23 = (f32[1,512]{1,0:T(1,128)S(1)}, f32[1,512]{1,0:T(1,128)}, u32[]{:S(2)}) copy-start(f32[1,512]{1,0:T(1,128)} %get-tuple-element.20) | copy-start | bytes 6148
  89.4 13.3 %all-to-all-start.2 = ((bf16[32,8,512]{2,1,0:T(8,128)(2,1)}), bf16[32,8,512]{2,1,0:T(8,128)(2,1)S(1)}, u32[]{:S(2)}, u32[]{:S(2)}) async-start(bf16[32,8,512]{2,1,0:T(8,128)(2,1)} %bitcast.23), calls=%async_computation.2 | async-start | bytes 524288 | tf_op jit(solution)/shard_map/all_to_all | solution.py:31
  110.4 4.9 %copy-start.33 = (f32[1,512]{1,0:T(1,128)S(1)}, f32[1,512]{1,0:T(1,128)}, u32[]{:S(2)}) copy-start(f32[1,512]{1,0:T(1,128)} %get-tuple-element.18) | copy-start | bytes 6148
  136.6 6.0 %copy-start.9 = (f32[320,512]{1,0:T(8,128)S(1)}, f32[320,512]{1,0:T(8,128)}, u32[]{:S(2)}) copy-start(f32[320,512]{1,0:T(8,128)} %convolution_add_fusion.1) | copy-start | bytes 1966084
  136.6 6.0 %copy-start.38 = (s32[2560]{0:T(1024)S(1)}, s32[2560]{0:T(1024)}, u32[]{:S(2)}) copy-start(s32[2560]{0:T(1024)} %param.19) | copy-start | bytes 30724
  142.6 4.2 %copy-start.8 = (bf16[2,512,512]{2,1,0:T(8,128)(2,1)S(1)}, bf16[2,512,512]{2,1,0:T(8,128)(2,1)}, u32[]{:S(2)}) copy-start(bf16[2,512,512]{2,1,0:T(8,128)(2,1)} %param.29) | copy-start | bytes 3145732
  142.6 4.9 %copy-start.4 = (f32[2,40,8,256]{3,2,0,1:T(8,128)S(1)}, f32[2,40,8,256]{3,2,0,1:T(8,128)}, u32[]{:S(2)}) copy-start(f32[2,40,8,256]{3,2,0,1:T(8,128)} %copy-done.2) | copy-start | bytes 1966084
  142.6 4.9 %copy-start.6 = (f32[320,512]{1,0:T(8,128)S(1)}, f32[320,512]{1,0:T(8,128)}, u32[]{:S(2)}) copy-start(f32[320,512]{1,0:T(8,128)} %copy-done.5) | copy-start | bytes 1966084
  142.6 4.9 %copy-start.12 = (f32[320]{0:T(512)S(1)}, f32[320]{0:T(512)}, u32[]{:S(2)}) copy-start(f32[320]{0:T(512)} %copy-done.11) | copy-start | bytes 3844
  142.6 4.9 %copy-start.16 = (f32[320]{0:T(512)S(1)}, f32[320]{0:T(512)}, u32[]{:S(2)}) copy-start(f32[320]{0:T(512)} %copy-done.15) | copy-start | bytes 3844
  142.6 4.9 %copy-start.18 = (f32[1,512]{1,0:T(1,128)S(1)}, f32[1,512]{1,0:T(1,128)}, u32[]{:S(2)}) copy-start(f32[1,512]{1,0:T(1,128)} %get-tuple-element.11) | copy-start | bytes 6148
  142.6 4.9 %copy-start.20 = (f32[1,512]{1,0:T(1,128)S(1)}, f32[1,512]{1,0:T(1,128)}, u32[]{:S(2)}) copy-start(f32[1,512]{1,0:T(1,128)} %get-tuple-element.13) | copy-start | bytes 6148
  142.6 4.9 %copy-start.21 = (f32[1,512]{1,0:T(1,128)S(1)}, f32[1,512]{1,0:T(1,128)}, u32[]{:S(2)}) copy-start(f32[1,512]{1,0:T(1,128)} %get-tuple-element.10) | copy-start | bytes 6148
  142.6 4.9 %copy-start.22 = (f32[1,512]{1,0:T(1,128)S(1)}, f32[1,512]{1,0:T(1,128)}, u32[]{:S(2)}) copy-start(f32[1,512]{1,0:T(1,128)} %get-tuple-element.12) | copy-start | bytes 6148
  (10 other events, 34.0 us)
where the time goes:
time: 150 us; the launch traced here: 149 us
  matrix products  64.7 us (43%)
  local copies, waits for them, and re-layouts  38.7 us (26%)
  other arithmetic  23 us (15%)
  starting transfers between devices  14.2 us (9%)
  waiting for transfers between devices  7.02 us (5%)
    dot_general x8, matrix products, perceptron(): jnp.dot(pieces[position], first_weight[position * columns:(position + 1)...  35.5 us
    dot_general x4, matrix products, perceptron(): result = jnp.dot(active, second_weight, preferred_element_type=jnp.float32)  23 us
    gather x2, local copies, waits for them, and re-layouts, shards(): sender_table[edge_sender]  15.5 us
    unnamed x80, local copies, waits for them, and re-layouts  14.9 us
    add x2, other arithmetic, shards(): edge_state + jnp.where(usable[:, None], update, jnp.zeros_like(update))  12.5 us
    all_to_all x2, starting transfers between devices, fetch_halo(): lax.all_to_all(outgoing, ('patch', 'band'), split_axis=0, concat_axis=0,...  9.93 us
    all_to_all x2, waiting for transfers between devices, fetch_halo(): lax.all_to_all(outgoing, ('patch', 'band'), split_axis=0, concat_axis=0,...  7.02 us
    reduce_sum x4, other arithmetic, layer_norm(): spread = jnp.mean(centre * centre, axis=-1, keepdims=True)  6.93 us
  transfers between devices with their start and end apart: 3, of which 2 were waited for; matrix products, arithmetic and copies ran while one was open for 22% of the time, Pallas kernels for 0%

commit v1 on v0

v1 whole, which is shorter than its diff:
```python
import functools

import jax
import jax.numpy as jnp
from jax import lax
from jax.experimental import pallas as pl
from jax.experimental.pallas import tpu as pltpu
from jax.sharding import PartitionSpec as P

epsilon = 1e-05
MESH = pl.DeviceIdType.MESH
F32 = jnp.float32
BF16 = jnp.bfloat16


def dot(a, b):
    return jnp.dot(a, b, preferred_element_type=F32)


def layer_norm(values, gain, offset):
    centre = values - jnp.mean(values, axis=-1, keepdims=True)
    spread = jnp.mean(centre * centre, axis=-1, keepdims=True)
    return centre * lax.rsqrt(spread + epsilon) * gain + offset


def swish(v):
    return (v * jax.nn.sigmoid(v)).astype(BF16)


def one_hot(column, width):
    places = lax.broadcasted_iota(jnp.int32, (column.shape[0], width), 1)
    return jnp.where(places == column, 1.0, 0.0).astype(BF16)


def one_hot_rows(row, height):
    places = lax.broadcasted_iota(jnp.int32, (height, row.shape[1]), 0)
    return jnp.where(places == row, 1.0, 0.0).astype(BF16)


def local_hot(columns, nodes):
    sender, receiver = columns[:, 0:1], columns[:, 1:2]
    local = jnp.where(sender < nodes, sender, -1)
    places = lax.broadcasted_iota(jnp.int32, (columns.shape[0], 2 * nodes), 1)
    hit = (places == local) | (places == receiver + nodes)
    return jnp.where(hit, 1.0, 0.0).astype(BF16)


def finish_edges(pre, state, columns, row, halo_table, second, gain, offset, nodes):
    pre = pre + dot(one_hot(columns[:, 0:1] - nodes, halo_table.shape[0]), halo_table)
    update = layer_norm(dot(swish(pre), second), gain, offset)
    state = state + jnp.where(columns[:, 2:3] > 0, update, jnp.zeros_like(update))
    return state, dot(one_hot_rows(row, nodes), state.astype(BF16))


def node_update(node_low, summed, first, first_bias, second, gain, offset):
    width = node_low.shape[1]
    v = dot(node_low, first[0:width]) + dot(summed.astype(BF16), first[width:]) + first_bias
    return layer_norm(dot(swish(v), second), gain, offset)


def first_kernel(
    patches, bands, chunk,
    lat_ref, columns_ref, rows_ref, lists_ref, eb_ref, eg_ref, eo_ref, nb_ref, ng_ref, no_ref,
    edge_hbm, ew1_hbm, ew2_hbm, nw1_hbm, nw2_hbm,
    node_out, table_out, state_hbm, pre_hbm,
    state, pre, w1, w2, v1, v2, x1, low_out, low_in, wide_in, out_a, out_b, in_a, in_b, table, summed,
    load_sem, store_sem, low_send, low_recv, wide_send, wide_recv, send_a, recv_a, send_b, recv_b,
):
    shards = patches * bands
    patch, band = lax.axis_index("patch"), lax.axis_index("band")
    me = patch * bands + band
    nodes = node_out.shape[0]
    edges, width = state.shape
    chunks = edges // chunk
    slot = out_a.shape[1]

    loads = [
        pltpu.make_async_copy(src, dst, load_sem.at[i])
        for i, (src, dst) in enumerate((
            (edge_hbm, state), (ew1_hbm.at[0], w1), (ew2_hbm.at[0], w2),
            (nw1_hbm.at[0], v1), (nw2_hbm.at[0], v2), (ew1_hbm.at[1], x1),
        ))
    ]
    for load in (loads[1], loads[0], loads[2], loads[3], loads[4], loads[5]):
        load.start()

    def place(q):
        return (lax.div(q, bands), lax.rem(q, bands))

    barrier = pltpu.get_barrier_semaphore()

    def greet(i, c):
        pl.semaphore_signal(barrier, inc=1, device_id=place(lax.rem(me + i, shards)), device_id_type=MESH)
        return c

    lax.fori_loop(1, shards, greet, 0)
    low_out[...] = lat_ref[...].astype(BF16)
    mine = pl.ds(pl.multiple_of(band * nodes, nodes), nodes)
    low_in[band] = lat_ref[mine, :].astype(BF16)
    wide_in[band] = lat_ref[mine, :]
    pl.semaphore_wait(barrier, shards - 1)

    exchanges = []
    for src, dst, ss, rs in ((low_out, low_in, low_send, low_recv), (lat_ref, wide_in, wide_send, wide_recv)):
        group = []
        for i in range(1, bands):
            other = lax.rem(band + i, bands)
            copy = pltpu.make_async_remote_copy(
                src_ref=src.at[pl.ds(pl.multiple_of(other * nodes, nodes), nodes)],
                dst_ref=dst.at[band],
                send_sem=ss.at[i],
                recv_sem=rs.at[i],
                device_id=(patch, other),
                device_id_type=MESH,
            )
            copy.start()
            group.append(copy)
        exchanges.append(group)

    def part(c):
        return pl.ds(pl.multiple_of(c * chunk, chunk), chunk)

    loads[1].wait()
    loads[0].wait()

    def own_edges(c, carry):
        pre[part(c), :] = dot(state[part(c), :].astype(BF16), w1[0:width, :]) + eb_ref[0:1, :]
        return carry

    lax.fori_loop(0, chunks, own_edges, 0)

    for copy in exchanges[0]:
        copy.wait()
    node_low = jnp.concatenate([low_in[i] for i in range(bands)], axis=1)
    hot_lists = one_hot_rows(lists_ref[...], nodes)

    def transfer(i, out, inn, ss, rs):
        q = lax.rem(me + i, shards)
        return pltpu.make_async_remote_copy(
            src_ref=out.at[q],
            dst_ref=inn.at[me],
            send_sem=ss.at[i],
            recv_sem=rs.at[i],
            device_id=place(q),
            device_id_type=MESH,
        )

    def send_halo(node_low, out, inn, ss, rs):
        picked = lax.dot_general(hot_lists, node_low, (((0,), (0,)), ((), ())), preferred_element_type=F32)
        out[...] = picked.reshape(shards, slot, width).astype(BF16)
        inn[me] = out[me]

        def go(i, c):
            transfer(i, out, inn, ss, rs).start()
            return c

        lax.fori_loop(1, shards, go, 0)

    def await_halo(out, inn, ss, rs):
        def stop(i, c):
            transfer(i, out, inn, ss, rs).wait()
            return c

        lax.fori_loop(1, shards, stop, 0)
        return inn[...].astype(F32).reshape(shards * slot, width).astype(BF16)

    send_halo(node_low, out_a, in_a, send_a, recv_a)
    table[0:nodes, :] = dot(node_low, w1[width : 2 * width, :]).astype(BF16)
    table[nodes:, :] = dot(node_low, w1[2 * width :, :]).astype(BF16)

    def own_nodes(c, carry):
        pre[part(c), :] += dot(local_hot(columns_ref[part(c), :], nodes), table[...])
        return carry

    lax.fori_loop(0, chunks, own_nodes, 0)
    for load in loads[2:]:
        load.wait()
    halo = await_halo(out_a, in_a, send_a, recv_a)
    table_out[...] = dot(halo, w1[width : 2 * width, :]).astype(BF16)
    summed[...] = jnp.zeros_like(summed)

    def finish(c, carry):
        fresh, added = finish_edges(
            pre[part(c), :], state[part(c), :], columns_ref[part(c), :], rows_ref[c], table_out[...],
            w2[...], eg_ref[0:1, :], eo_ref[0:1, :], nodes,
        )
        state[part(c), :] = fresh
        summed[...] += added
        return carry

    lax.fori_loop(0, chunks, finish, 0)
    for copy in exchanges[1]:
        copy.wait()
    node_state = jnp.concatenate([wide_in[i] for i in range(bands)], axis=1) + node_update(
        node_low, summed[...], v1, nb_ref[0:1, :], v2[...], ng_ref[0:1, :], no_ref[0:1, :]
    )
    node_out[...] = node_state
    node_low = node_state.astype(BF16)
    send_halo(node_low, out_b, in_b, send_b, recv_b)
    save_state = pltpu.make_async_copy(state, state_hbm, store_sem.at[0])
    save_state.start()
    table[0:nodes, :] = dot(node_low, x1[width : 2 * width, :]).astype(BF16)
    table[nodes:, :] = dot(node_low, x1[2 * width :, :]).astype(BF16)

    def begin(c, carry):
        pre[part(c), :] = (
            dot(state[part(c), :].astype(BF16), x1[0:width, :])
            + eb_ref[1:2, :]
            + dot(local_hot(columns_ref[part(c), :], nodes), table[...])
        )
        return carry

    lax.fori_loop(0, chunks, begin, 0)
    save_pre = pltpu.make_async_copy(pre, pre_hbm, store_sem.at[1])
    save_pre.start()
    halo = await_halo(out_b, in_b, send_b, recv_b)
    table_out[...] = dot(halo, x1[width : 2 * width, :]).astype(BF16)
    save_state.wait()
    save_pre.wait()


def second_kernel(
    chunks,
    pre_ref, state_ref, columns_ref, rows_ref, table_ref, ew2_ref, eg_ref, eo_ref,
    node_ref, nw1_ref, nb_ref, nw2_ref, ng_ref, no_ref,
    nodes_out, edges_out,
    summed,
):
    step = pl.program_id(0)
    nodes = node_ref.shape[0]

    @pl.when(step == 0)
    def _():
        summed[...] = jnp.zeros_like(summed)

    fresh, added = finish_edges(
        pre_ref[...], state_ref[...], columns_ref[...], rows_ref[0], table_ref[...],
        ew2_ref[0], eg_ref[1:2, :], eo_ref[1:2, :], nodes,
    )
    edges_out[...] = fresh
    summed[...] += added

    @pl.when(step == chunks - 1)
    def _():
        old = node_ref[...]
        nodes_out[...] = old + node_update(
            old.astype(BF16), summed[...], nw1_ref.at[0], nb_ref[1:2, :], nw2_ref[0], ng_ref[1:2, :], no_ref[1:2, :]
        )


def shards_body(
    patches, bands,
    latents, edge_latents, edge_sender, edge_receiver, block_counts, send_rows,
    edge_first_weight, edge_first_bias, edge_second_weight, edge_gain, edge_offset,
    node_first_weight, node_first_bias, node_second_weight, node_gain, node_offset,
):
    shards = patches * bands
    edges, width = edge_latents.shape
    block = edges // block_counts.shape[0]
    nodes = latents.shape[0] // bands
    slot = send_rows.shape[2]
    chunk = next(c for c in (512, 256, 128, block) if edges % c == 0)
    chunks = edges // chunk
    usable = (jnp.arange(block, dtype=jnp.int32)[None, :] < block_counts[:, None]).reshape(-1)
    columns = jnp.stack([edge_sender, edge_receiver, usable.astype(jnp.int32)], axis=1)
    rows = jnp.where(usable, edge_receiver, -1).reshape(chunks, 1, chunk)
    lists = send_rows.reshape(1, shards * slot)
    vmem, anywhere = pl.BlockSpec(memory_space=pltpu.VMEM), pl.BlockSpec(memory_space=pl.ANY)
    dma = pltpu.SemaphoreType.DMA
    half = latents.shape[1]
    node_state, table, state, pre = pl.pallas_call(
        functools.partial(first_kernel, patches, bands, chunk),
        out_shape=(
            jax.ShapeDtypeStruct((nodes, width), F32),
            jax.ShapeDtypeStruct((shards * slot, width), BF16),
            jax.ShapeDtypeStruct((edges, width), F32),
            jax.ShapeDtypeStruct((edges, width), F32),
        ),
        in_specs=[vmem] * 10 + [anywhere] * 5,
        out_specs=(vmem, vmem, anywhere, anywhere),
        scratch_shapes=[
            pltpu.VMEM((edges, width), F32),
            pltpu.VMEM((edges, width), F32),
            pltpu.VMEM(edge_first_weight.shape[1:], BF16),
            pltpu.VMEM(edge_second_weight.shape[1:], BF16),
            pltpu.VMEM(node_first_weight.shape[1:], BF16),
            pltpu.VMEM(node_second_weight.shape[1:], BF16),
            pltpu.VMEM(edge_first_weight.shape[1:], BF16),
            pltpu.VMEM(latents.shape, BF16),
            pltpu.VMEM((bands, nodes, half), BF16),
            pltpu.VMEM((bands, nodes, half), F32),
            pltpu.VMEM((shards, slot, width), BF16),
            pltpu.VMEM((shards, slot, width), BF16),
            pltpu.VMEM((shards, slot, width), BF16),
            pltpu.VMEM((shards, slot, width), BF16),
            pltpu.VMEM((2 * nodes, width), BF16),
            pltpu.VMEM((nodes, width), F32),
            dma((6,)), dma((2,)),
            dma((bands,)), dma((bands,)), dma((bands,)), dma((bands,)),
            dma((shards,)), dma((shards,)), dma((shards,)), dma((shards,)),
        ],
        compiler_params=pltpu.CompilerParams(
            collective_id=0, has_side_effects=True, vmem_limit_bytes=48 * 2**20
        ),
        name="layer_one",
    )(
        latents, columns, rows, lists, edge_first_bias, edge_gain, edge_offset,
        node_first_bias, node_gain, node_offset,
        edge_latents, edge_first_weight, edge_second_weight, node_first_weight, node_second_weight,
    )

    def whole(array):
        return pl.BlockSpec(array.shape, lambda c: (0,) * array.ndim)

    def second(array):
        return pl.BlockSpec((1,) + array.shape[1:], lambda c: (1, 0, 0))

    def stream(columns):
        return pl.BlockSpec((chunk, columns), lambda c: (c, 0))

    return pl.pallas_call(
        functools.partial(second_kernel, chunks),
        grid=(chunks,),
        out_shape=(
            jax.ShapeDtypeStruct((nodes, width), F32),
            jax.ShapeDtypeStruct((edges, width), F32),
        ),
        in_specs=[
            stream(width), stream(width), stream(3), pl.BlockSpec((1, 1, chunk), lambda c: (c, 0, 0)),
            whole(table), second(edge_second_weight), whole(edge_gain), whole(edge_offset),
            whole(node_state), second(node_first_weight), whole(node_first_bias), second(node_second_weight),
            whole(node_gain), whole(node_offset),
        ],
        out_specs=(whole(node_state), stream(width)),
        scratch_shapes=[pltpu.VMEM((nodes, width), F32)],
        compiler_params=pltpu.CompilerParams(
            dimension_semantics=("arbitrary",), vmem_limit_bytes=48 * 2**20
        ),
        name="layer_two",
    )(
        pre, state, columns, rows, table, edge_second_weight, edge_gain, edge_offset,
        node_state, node_first_weight, node_first_bias, node_second_weight, node_gain, node_offset,
    )


def solution(mesh):
    owned = P(("patch", "band"))
    return jax.shard_map(
        functools.partial(shards_body, mesh.shape["patch"], mesh.shape["band"]),
        mesh=mesh,
        in_specs=(P("patch", "band"), owned, owned, owned, owned, owned) + (P(),) * 10,
        out_specs=(owned, owned),
        check_vma=False,
    )
```

time: 150 us -> 63.2 us (0.42)
  matrix products: 64.7 us -> 0 us
  Pallas kernels: 0 us -> 49.9 us
  local copies, waits for them, and re-layouts: 38.7 us -> 10.4 us
  other arithmetic: 23 us -> 1.54 us
  starting transfers between devices: 14.2 us -> 0 us
  waiting for transfers between devices: 7.02 us -> 0 us
    dot_general x14 -> x0, matrix products: 64.7 us -> none  [the longest x8 35.5 us: perceptron(): jnp.dot(pieces[position], first_weight[position * columns:(position + 1)...]
    pallas_call x0 -> x2, Pallas kernels: none -> 49.9 us  [the longest x1 38.3 us: shards_body(): pl.pallas_call(functools.partial(first_kernel, patches, bands, chunk), ou...]
    gather x4 -> x0, local copies, waits for them, and re-layouts: 19.2 us -> none  [the longest x2 15.5 us: shards(): sender_table[edge_sender]]
    all_to_all x3 -> x0, starting transfers between devices: 14.2 us -> none  [the longest x2 9.93 us: fetch_halo(): lax.all_to_all(outgoing, ('patch', 'band'), split_axis=0, concat_axis=0,...]
    add x3 -> x0, other arithmetic: 13.6 us -> none  [the longest x2 12.5 us: shards(): edge_state + jnp.where(usable[:, None], update, jnp.zeros_like(update))]
    all_to_all x3 -> x0, waiting for transfers between devices: 7.02 us -> none  [the longest x2 7.02 us: fetch_halo(): lax.all_to_all(outgoing, ('patch', 'band'), split_axis=0, concat_axis=0,...]
    reduce_sum x4 -> x0, other arithmetic: 6.93 us -> none  [layer_norm(): spread = jnp.mean(centre * centre, axis=-1, keepdims=True)]
    unnamed x80 -> x24, local copies, waits for them, and re-layouts: 14.9 us -> 8.44 us
  transfers between devices with their start and end apart: 3 -> 0, of which waited for: 2 -> 0; matrix products, arithmetic and copies ran while one was open for 22% -> 0% of each run, Pallas kernels for 0% -> 0%
where the time goes in v1:
time: 63.2 us; the launch traced here: 62.5 us
  Pallas kernels  49.9 us (79%)
  local copies, waits for them, and re-layouts  10.4 us (16%)
  other arithmetic  1.54 us (2%)
  between operations  0.69 us (1%)
    pallas_call x1, Pallas kernels, shards_body(): pl.pallas_call(functools.partial(first_kernel, patches, bands, chunk), ou...  38.3 us
    pallas_call x1, Pallas kernels, shards_body(): pl.pallas_call(functools.partial(second_kernel, chunks), grid=(chunks,),...  11.5 us
    unnamed x24, local copies, waits for them, and re-layouts  8.44 us
    another operation x3, local copies, waits for them, and re-layouts, shards_body(): jnp.stack([edge_sender, edge_receiver, usable.astype(jnp.int32)], axis=1)  1.86 us

profile of v1, /device:TPU:0, one launch (start us, length us, event | category | flops | bytes accessed | tf_op | source)
XLA Modules:
  0.0 62.5 jit_solution(5039425100552997094)
XLA Ops:
  0.6 0.7 %stack.10 = s32[2560,1]{0,1:T(1,128)S(1)} reshape(s32[2560]{0:T(1024)} %param.18) | data formatting | bytes 20480 | tf_op jit(solution)/shard_map/stack | solution.py:265
  1.3 0.7 %stack.11 = s32[2560,1]{0,1:T(1,128)S(1)} reshape(s32[2560]{0:T(1024)} %param.19) | data formatting | bytes 20480 | tf_op jit(solution)/shard_map/stack | solution.py:265
  2.1 0.8 %fusion.1 = s32[2560]{0:T(1024)S(1)} fusion(s32[2560]{0:T(1024)} %param.19, s32[20]{0:T(128)} %param.20), kind=kLoop, calls=%fused_computation.4 | loop fusion | flops 5120 | bytes 20560 | tf_op jit(solution)/shard_map/jit(_where)/select_n | solution.py:266
  2.9 0.7 %convert_bitcast_fusion = s32[1,1,20,128]{3,2,1,0:T(8,128)S(1)} fusion(s32[20]{0:T(128)} %param.20), kind=kLoop, calls=%fused_computation.1 | loop fusion | flops 5120 | bytes 10320
  3.6 0.8 %copy.23 = s32[1,32,8]{2,1,0:T(8,128)S(1)} copy(s32[1,32,8]{1,2,0:T(8,128)} %param.21) | data formatting | bytes 2048 | tf_op args[5]
  4.4 0.1 reshape.39.lists_ref
  4.5 0.4 copy.24.columns_ref
  4.9 0.0 copy-start
  4.9 1.2 %copy-done = bf16[2,512,512]{2,1,0:T(8,128)(2,1)S(1)} copy-done((bf16[2,512,512]{2,1,0:T(8,128)(2,1)S(1)}, bf16[2,512,512]{2,1,0:T(8,128)(2,1)}, u32[]{:S(2)}) %copy-start) | copy-done | bytes 1048600
  6.2 0.0 copy-start.2
  6.2 1.2 %copy-done.2 = bf16[2,512,512]{2,1,0:T(8,128)(2,1)S(1)} copy-done((bf16[2,512,512]{2,1,0:T(8,128)(2,1)S(1)}, bf16[2,512,512]{2,1,0:T(8,128)(2,1)}, u32[]{:S(2)}) %copy-start.2) | copy-done | bytes 1048600
  7.4 0.0 copy-start.4
  7.4 1.1 %copy-done.4 = f32[640,256]{1,0:T(8,128)S(1)} copy-done((f32[640,256]{1,0:T(8,128)S(1)}, f32[640,256]{1,0:T(8,128)}, u32[]{:S(2)}) %copy-start.4) | copy-done | bytes 655384
  8.5 0.0 copy-start.5
  8.5 0.7 %copy-done.5 = f32[2,512]{1,0:T(2,128)S(1)} copy-done((f32[2,512]{1,0:T(2,128)S(1)}, f32[2,512]{1,0:T(2,128)}, u32[]{:S(2)}) %copy-start.5) | copy-done | bytes 4120
  9.2 0.0 copy-start.6
  9.2 0.7 %copy-done.6 = f32[2,512]{1,0:T(2,128)S(1)} copy-done((f32[2,512]{1,0:T(2,128)S(1)}, f32[2,512]{1,0:T(2,128)}, u32[]{:S(2)}) %copy-start.6) | copy-done | bytes 4120
  9.9 0.0 copy-start.7
  9.9 0.7 %copy-done.7 = f32[2,512]{1,0:T(2,128)S(1)} copy-done((f32[2,512]{1,0:T(2,128)S(1)}, f32[2,512]{1,0:T(2,128)}, u32[]{:S(2)}) %copy-start.7) | copy-done | bytes 4120
  10.5 0.0 copy-start.8
  10.5 0.7 %copy-done.8 = f32[2,512]{1,0:T(2,128)S(1)} copy-done((f32[2,512]{1,0:T(2,128)S(1)}, f32[2,512]{1,0:T(2,128)}, u32[]{:S(2)}) %copy-start.8) | copy-done | bytes 4120
  11.2 0.0 copy-start.9
  11.2 0.7 %copy-done.9 = f32[2,512]{1,0:T(2,128)S(1)} copy-done((f32[2,512]{1,0:T(2,128)S(1)}, f32[2,512]{1,0:T(2,128)}, u32[]{:S(2)}) %copy-start.9) | copy-done | bytes 4120
  11.9 0.0 copy-start.10
  11.9 0.7 %copy-done.10 = f32[2,512]{1,0:T(2,128)S(1)} copy-done((f32[2,512]{1,0:T(2,128)S(1)}, f32[2,512]{1,0:T(2,128)}, u32[]{:S(2)}) %copy-start.10) | copy-done | bytes 4120
  12.6 0.0 copy-start.1
  12.6 0.0 copy-start.3
  12.6 38.3 %layer_one.1 = (f32[320,512]{1,0:T(8,128)S(1)}, bf16[256,512]{1,0:T(8,128)(2,1)S(1)}, f32[2560,512]{1,0:T(8,128)}, f32[2560,512]{1,0:T(8,128)}) custom-call(f32[640,256]{1,0:T(8,128)S(1)} %copy-done.4, s32[2560,3]{1,0:T(8,128)S(1)} %copy.24.columns_ref, s32[5,1,512]{2,1,0:T(1,128)S(1)} %reshape.38.rows_ref, s32[1,256]{1,0:T(1,128)S(1)} %reshape.39.lists_ref, ...), custom_call_target="tpu_custom_call" | custom-call | tf_op jit(solution)/shard_map/layer_one/pallas_call | solution.py:271
  51.0 0.0 copy-done.1
  51.0 0.0 copy-done.3
  51.0 11.5 %layer_two.1 = (f32[320,512]{1,0:T(8,128)}, f32[2560,512]{1,0:T(8,128)}) custom-call(f32[2560,512]{1,0:T(8,128)} %get-tuple-element.6.pre_ref, f32[2560,512]{1,0:T(8,128)} %get-tuple-element.7.state_ref, s32[2560,3]{1,0:T(8,128)S(1)} %copy.24.columns_ref, s32[5,1,512]{2,1,0:T(1,128)S(1)} %reshape.38.rows_ref, ...), custom_call_target="tpu_custom_call" | custom-call | tf_op jit(solution)/shard_map/layer_two/pallas_call | solution.py:321
  (3 shorter events, 0.1 us)
Async XLA Ops:
  4.9 1.2 %copy-start = (bf16[2,512,512]{2,1,0:T(8,128)(2,1)S(1)}, bf16[2,512,512]{2,1,0:T(8,128)(2,1)}, u32[]{:S(2)}) copy-start(bf16[2,512,512]{2,1,0:T(8,128)(2,1)} %ew2_ref.1) | copy-start | bytes 3145732
  6.2 1.2 %copy-start.2 = (bf16[2,512,512]{2,1,0:T(8,128)(2,1)S(1)}, bf16[2,512,512]{2,1,0:T(8,128)(2,1)}, u32[]{:S(2)}) copy-start(bf16[2,512,512]{2,1,0:T(8,128)(2,1)} %nw2_ref.1) | copy-start | bytes 3145732
  7.4 1.1 %copy-start.4 = (f32[640,256]{1,0:T(8,128)S(1)}, f32[640,256]{1,0:T(8,128)}, u32[]{:S(2)}) copy-start(f32[640,256]{1,0:T(8,128)} %lat_ref.1) | copy-start | bytes 1966084
  8.5 0.7 %copy-start.5 = (f32[2,512]{1,0:T(2,128)S(1)}, f32[2,512]{1,0:T(2,128)}, u32[]{:S(2)}) copy-start(f32[2,512]{1,0:T(2,128)} %eg_ref.3) | copy-start | bytes 12292
  9.2 0.7 %copy-start.6 = (f32[2,512]{1,0:T(2,128)S(1)}, f32[2,512]{1,0:T(2,128)}, u32[]{:S(2)}) copy-start(f32[2,512]{1,0:T(2,128)} %eo_ref.3) | copy-start | bytes 12292
  9.9 0.7 %copy-start.7 = (f32[2,512]{1,0:T(2,128)S(1)}, f32[2,512]{1,0:T(2,128)}, u32[]{:S(2)}) copy-start(f32[2,512]{1,0:T(2,128)} %nb_ref.3) | copy-start | bytes 12292
  10.5 0.7 %copy-start.8 = (f32[2,512]{1,0:T(2,128)S(1)}, f32[2,512]{1,0:T(2,128)}, u32[]{:S(2)}) copy-start(f32[2,512]{1,0:T(2,128)} %ng_ref.3) | copy-start | bytes 12292
  11.2 0.7 %copy-start.9 = (f32[2,512]{1,0:T(2,128)S(1)}, f32[2,512]{1,0:T(2,128)}, u32[]{:S(2)}) copy-start(f32[2,512]{1,0:T(2,128)} %no_ref.3) | copy-start | bytes 12292
  11.9 0.7 %copy-start.10 = (f32[2,512]{1,0:T(2,128)S(1)}, f32[2,512]{1,0:T(2,128)}, u32[]{:S(2)}) copy-start(f32[2,512]{1,0:T(2,128)} %eb_ref.1) | copy-start | bytes 12292
  12.6 38.4 %copy-start.1 = (bf16[2,512,512]{2,1,0:T(8,128)(2,1)S(1)}, bf16[2,512,512]{2,1,0:T(8,128)(2,1)}, u32[]{:S(2)}) copy-start(bf16[2,512,512]{2,1,0:T(8,128)(2,1)} %ew2_ref.1) | copy-start | bytes 3145732
  12.6 38.4 %copy-start.3 = (bf16[2,512,512]{2,1,0:T(8,128)(2,1)S(1)}, bf16[2,512,512]{2,1,0:T(8,128)(2,1)}, u32[]{:S(2)}) copy-start(bf16[2,512,512]{2,1,0:T(8,128)(2,1)} %nw2_ref.1) | copy-start | bytes 3145732

commit v2 on v1

--- a/solution.py
+++ b/solution.py
@@ -27,9 +27,18 @@
     return (v * jax.nn.sigmoid(v)).astype(BF16)
 
 
-def one_hot(column, width):
-    places = lax.broadcasted_iota(jnp.int32, (column.shape[0], width), 1)
-    return jnp.where(places == column, 1.0, 0.0).astype(BF16)
+LANES = 128
+
+
+def hot_columns(conditions, width):
+    places = lax.broadcasted_iota(jnp.int32, (conditions[0].shape[0], LANES), 1)
+    pieces = []
+    for first in range(0, width, LANES):
+        hit = places == conditions[0] - first
+        for other in conditions[1:]:
+            hit = hit | (places == other - first)
+        pieces.append(jnp.where(hit, 1.0, 0.0))
+    return jnp.concatenate(pieces, axis=1).astype(BF16)
 
 
 def one_hot_rows(row, height):
@@ -37,18 +46,34 @@
     return jnp.where(places == row, 1.0, 0.0).astype(BF16)
 
 
-def local_hot(columns, nodes):
-    sender, receiver = columns[:, 0:1], columns[:, 1:2]
-    local = jnp.where(sender < nodes, sender, -1)
-    places = lax.broadcasted_iota(jnp.int32, (columns.shape[0], 2 * nodes), 1)
-    hit = (places == local) | (places == receiver + nodes)
-    return jnp.where(hit, 1.0, 0.0).astype(BF16)
-
-
-def finish_edges(pre, state, columns, row, halo_table, second, gain, offset, nodes):
-    pre = pre + dot(one_hot(columns[:, 0:1] - nodes, halo_table.shape[0]), halo_table)
+def hot_columns_of(rows, width, step):
+    row_place = lax.broadcasted_iota(jnp.int32, (rows, width), 0)
+    column_place = lax.broadcasted_iota(jnp.int32, (rows, width), 1)
+    return jnp.where(lax.div(row_place, step) == column_place, 1.0, 0.0).astype(BF16)
+
+
+def to_columns(row):
+    return jnp.broadcast_to(row, (row.shape[1], row.shape[1])).T
+
+
+def used_row(row, count):
+    places = lax.broadcasted_iota(jnp.int32, row.shape, 1)
+    return jnp.where(places < count, row, -1)
+
+
+def local_hot(sender, receiver, nodes):
+    return hot_columns((jnp.where(sender < nodes, sender, -1), receiver + nodes), 2 * nodes)
+
+
+def finish_edges(pre, state, sender, row, counts, halo_table, second, gain, offset, nodes):
+    pre = pre + dot(hot_columns((sender - nodes,), halo_table.shape[0]), halo_table)
     update = layer_norm(dot(swish(pre), second), gain, offset)
-    state = state + jnp.where(columns[:, 2:3] > 0, update, jnp.zeros_like(update))
+    places = lax.broadcasted_iota(jnp.int32, (LANES, update.shape[1]), 0)
+    kept = [
+        jnp.where(places < count, update[i * LANES : (i + 1) * LANES], 0.0)
+        for i, count in enumerate(counts)
+    ]
+    state = state + jnp.concatenate(kept, axis=0)
     return state, dot(one_hot_rows(row, nodes), state.astype(BF16))
 
 
@@ -60,9 +85,12 @@
 
 def first_kernel(
     patches, bands, chunk,
-    lat_ref, columns_ref, rows_ref, lists_ref, eb_ref, eg_ref, eo_ref, nb_ref, ng_ref, no_ref,
+    counts_ref,
+    lat_hbm, senders_hbm, receivers_hbm, lists_hbm, eb_hbm, eg_hbm, eo_hbm, nb_hbm, ng_hbm, no_hbm,
     edge_hbm, ew1_hbm, ew2_hbm, nw1_hbm, nw2_hbm,
-    node_out, table_out, state_hbm, pre_hbm,
+    node_hbm, table_hbm, state_hbm, pre_hbm,
+    lat_ref, senders_ref, receivers_ref, lists_ref, eb_ref, eg_ref, eo_ref, nb_ref, ng_ref, no_ref,
+    node_out, table_out, sender_cols, receiver_cols, rows_ref,
     state, pre, w1, w2, v1, v2, x1, low_out, low_in, wide_in, out_a, out_b, in_a, in_b, table, summed,
     load_sem, store_sem, low_send, low_recv, wide_send, wide_recv, send_a, recv_a, send_b, recv_b,
 ):
@@ -72,6 +100,7 @@
     nodes = node_out.shape[0]
     edges, width = state.shape
     chunks = edges // chunk
+    blocks = chunk // LANES
     slot = out_a.shape[1]
 
     loads = [
@@ -79,9 +108,12 @@
         for i, (src, dst) in enumerate((
             (edge_hbm, state), (ew1_hbm.at[0], w1), (ew2_hbm.at[0], w2),
             (nw1_hbm.at[0], v1), (nw2_hbm.at[0], v2), (ew1_hbm.at[1], x1),
+            (lat_hbm, lat_ref), (senders_hbm, senders_ref), (receivers_hbm, receivers_ref),
+            (lists_hbm.at[0], lists_ref), (eb_hbm, eb_ref), (eg_hbm, eg_ref), (eo_hbm, eo_ref),
+            (nb_hbm, nb_ref), (ng_hbm, ng_ref), (no_hbm, no_ref),
         ))
     ]
-    for load in (loads[1], loads[0], loads[2], loads[3], loads[4], loads[5]):
+    for load in [loads[i] for i in (6, 7, 8, 9, 10, 1, 0, 2, 3, 4, 5, 11, 12, 13, 14, 15)]:
         load.start()
 
     def place(q):
@@ -94,6 +126,7 @@
         return c
 
     lax.fori_loop(1, shards, greet, 0)
+    loads[6].wait()
     low_out[...] = lat_ref[...].astype(BF16)
     mine = pl.ds(pl.multiple_of(band * nodes, nodes), nodes)
     low_in[band] = lat_ref[mine, :].astype(BF16)
@@ -120,6 +153,29 @@
     def part(c):
         return pl.ds(pl.multiple_of(c * chunk, chunk), chunk)
 
+    for load in loads[7:11]:
+        load.wait()
+
+    def turn(j, carry):
+        here = pl.ds(pl.multiple_of(j * LANES, LANES), LANES)
+        sender_cols[here, :] = to_columns(senders_ref[j])
+        receiver_cols[here, :] = to_columns(receivers_ref[j])
+        rows_ref[j] = used_row(receivers_ref[j], counts_ref[j])
+        return carry
+
+    lax.fori_loop(0, edges // LANES, turn, 0)
+    lists = lists_ref[...]
+    slots = lists.shape[1]
+    spread = hot_columns_of(shards * slots, shards, slots)
+    high = dot(spread, jnp.right_shift(lists, 4).astype(F32).astype(BF16))
+    picked_all = high * 16.0 + dot(spread, jnp.bitwise_and(lists, 15).astype(F32).astype(BF16))
+    row_place = lax.broadcasted_iota(jnp.int32, picked_all.shape, 0)
+    slot_place = lax.broadcasted_iota(jnp.int32, picked_all.shape, 1)
+    wanted = jnp.sum(
+        jnp.where(lax.rem(row_place, slots) == slot_place, picked_all, 0.0), axis=1, keepdims=True
+    )
+    node_place = lax.broadcasted_iota(jnp.int32, (shards * slots, nodes), 1).astype(F32)
+    hot_lists = jnp.where(node_place == wanted, 1.0, 0.0).astype(BF16)
     loads[1].wait()
     loads[0].wait()
 
@@ -132,7 +188,6 @@
     for copy in exchanges[0]:
         copy.wait()
     node_low = jnp.concatenate([low_in[i] for i in range(bands)], axis=1)
-    hot_lists = one_hot_rows(lists_ref[...], nodes)
 
     def transfer(i, out, inn, ss, rs):
         q = lax.rem(me + i, shards)
@@ -146,7 +201,7 @@
         )
 
     def send_halo(node_low, out, inn, ss, rs):
-        picked = lax.dot_general(hot_lists, node_low, (((0,), (0,)), ((), ())), preferred_element_type=F32)
+        picked = dot(hot_lists, node_low)
         out[...] = picked.reshape(shards, slot, width).astype(BF16)
         inn[me] = out[me]
 
@@ -169,11 +224,11 @@
     table[nodes:, :] = dot(node_low, w1[2 * width :, :]).astype(BF16)
 
     def own_nodes(c, carry):
-        pre[part(c), :] += dot(local_hot(columns_ref[part(c), :], nodes), table[...])
+        pre[part(c), :] += dot(local_hot(sender_cols[part(c), :], receiver_cols[part(c), :], nodes), table[...])
         return carry
 
     lax.fori_loop(0, chunks, own_nodes, 0)
-    for load in loads[2:]:
+    for load in loads[2:6] + loads[11:]:
         load.wait()
     halo = await_halo(out_a, in_a, send_a, recv_a)
     table_out[...] = dot(halo, w1[width : 2 * width, :]).astype(BF16)
@@ -181,7 +236,9 @@
 
     def finish(c, carry):
         fresh, added = finish_edges(
-            pre[part(c), :], state[part(c), :], columns_ref[part(c), :], rows_ref[c], table_out[...],
+            pre[part(c), :], state[part(c), :], sender_cols[part(c), :],
+            jnp.concatenate([rows_ref[c * blocks + i] for i in range(blocks)], axis=1),
+            [counts_ref[c * blocks + i] for i in range(blocks)], table_out[...],
             w2[...], eg_ref[0:1, :], eo_ref[0:1, :], nodes,
         )
         state[part(c), :] = fresh
@@ -195,6 +252,8 @@
         node_low, summed[...], v1, nb_ref[0:1, :], v2[...], ng_ref[0:1, :], no_ref[0:1, :]
     )
     node_out[...] = node_state
+    save_nodes = pltpu.make_async_copy(node_out, node_hbm, store_sem.at[2])
+    save_nodes.start()
     node_low = node_state.astype(BF16)
     send_halo(node_low, out_b, in_b, send_b, recv_b)
     save_state = pltpu.make_async_copy(state, state_hbm, store_sem.at[0])
@@ -206,7 +265,7 @@
         pre[part(c), :] = (
             dot(state[part(c), :].astype(BF16), x1[0:width, :])
             + eb_ref[1:2, :]
-            + dot(local_hot(columns_ref[part(c), :], nodes), table[...])
+            + dot(local_hot(sender_cols[part(c), :], receiver_cols[part(c), :], nodes), table[...])
         )
         return carry
 
@@ -215,13 +274,15 @@
     save_pre.start()
     halo = await_halo(out_b, in_b, send_b, recv_b)
     table_out[...] = dot(halo, x1[width : 2 * width, :]).astype(BF16)
-    save_state.wait()
-    save_pre.wait()
+    save_table = pltpu.make_async_copy(table_out, table_hbm, store_sem.at[3])
+    save_table.start()
+    for save in (save_nodes, save_state, save_pre, save_table):
+        save.wait()
 
 
 def second_kernel(
     chunks,
-    pre_ref, state_ref, columns_ref, rows_ref, table_ref, ew2_ref, eg_ref, eo_ref,
+    counts_ref, pre_ref, state_ref, senders_ref, receivers_ref, table_ref, ew2_ref, eg_ref, eo_ref,
     node_ref, nw1_ref, nb_ref, nw2_ref, ng_ref, no_ref,
     nodes_out, edges_out,
     summed,
@@ -233,8 +294,13 @@
     def _():
         summed[...] = jnp.zeros_like(summed)
 
+    blocks = senders_ref.shape[0]
+    counts = [counts_ref[step * blocks + i] for i in range(blocks)]
     fresh, added = finish_edges(
-        pre_ref[...], state_ref[...], columns_ref[...], rows_ref[0], table_ref[...],
+        pre_ref[...], state_ref[...],
+        jnp.concatenate([to_columns(senders_ref[i]) for i in range(blocks)], axis=0),
+        jnp.concatenate([used_row(receivers_ref[i], counts[i]) for i in range(blocks)], axis=1),
+        counts, table_ref[...],
         ew2_ref[0], eg_ref[1:2, :], eo_ref[1:2, :], nodes,
     )
     edges_out[...] = fresh
@@ -259,13 +325,11 @@
     block = edges // block_counts.shape[0]
     nodes = latents.shape[0] // bands
     slot = send_rows.shape[2]
-    chunk = next(c for c in (512, 256, 128, block) if edges % c == 0)
+    chunk = next(c for c in (512, 256, 128) if edges % c == 0 and block == LANES)
     chunks = edges // chunk
-    usable = (jnp.arange(block, dtype=jnp.int32)[None, :] < block_counts[:, None]).reshape(-1)
-    columns = jnp.stack([edge_sender, edge_receiver, usable.astype(jnp.int32)], axis=1)
-    rows = jnp.where(usable, edge_receiver, -1).reshape(chunks, 1, chunk)
-    lists = send_rows.reshape(1, shards * slot)
-    vmem, anywhere = pl.BlockSpec(memory_space=pltpu.VMEM), pl.BlockSpec(memory_space=pl.ANY)
+    senders = edge_sender.reshape(edges // LANES, 1, LANES)
+    receivers = edge_receiver.reshape(edges // LANES, 1, LANES)
+    scalars, anywhere = pl.BlockSpec(memory_space=pltpu.SMEM), pl.BlockSpec(memory_space=pl.ANY)
     dma = pltpu.SemaphoreType.DMA
     half = latents.shape[1]
     node_state, table, state, pre = pl.pallas_call(
@@ -276,9 +340,19 @@
             jax.ShapeDtypeStruct((edges, width), F32),
             jax.ShapeDtypeStruct((edges, width), F32),
         ),
-        in_specs=[vmem] * 10 + [anywhere] * 5,
-        out_specs=(vmem, vmem, anywhere, anywhere),
+        in_specs=[scalars] + [anywhere] * 15,
+        out_specs=(anywhere,) * 4,
         scratch_shapes=[
+            pltpu.VMEM(latents.shape, F32),
+            pltpu.VMEM(senders.shape, jnp.int32),
+            pltpu.VMEM(senders.shape, jnp.int32),
+            pltpu.VMEM(send_rows.shape[1:], jnp.int32),
+        ] + [pltpu.VMEM(edge_gain.shape, F32)] * 6 + [
+            pltpu.VMEM((nodes, width), F32),
+            pltpu.VMEM((shards * slot, width), BF16),
+            pltpu.VMEM((edges, LANES), jnp.int32),
+            pltpu.VMEM((edges, LANES), jnp.int32),
+            pltpu.VMEM(senders.shape, jnp.int32),
             pltpu.VMEM((edges, width), F32),
             pltpu.VMEM((edges, width), F32),
             pltpu.VMEM(edge_first_weight.shape[1:], BF16),
@@ -295,16 +369,16 @@
             pltpu.VMEM((shards, slot, width), BF16),
             pltpu.VMEM((2 * nodes, width), BF16),
             pltpu.VMEM((nodes, width), F32),
-            dma((6,)), dma((2,)),
+            dma((16,)), dma((4,)),
             dma((bands,)), dma((bands,)), dma((bands,)), dma((bands,)),
             dma((shards,)), dma((shards,)), dma((shards,)), dma((shards,)),
         ],
         compiler_params=pltpu.CompilerParams(
-            collective_id=0, has_side_effects=True, vmem_limit_bytes=48 * 2**20
+            collective_id=0, has_side_effects=True, vmem_limit_bytes=67043328
         ),
         name="layer_one",
     )(
-        latents, columns, rows, lists, edge_first_bias, edge_gain, edge_offset,
+        block_counts, latents, senders, receivers, send_rows, edge_first_bias, edge_gain, edge_offset,
         node_first_bias, node_gain, node_offset,
         edge_latents, edge_first_weight, edge_second_weight, node_first_weight, node_second_weight,
     )
@@ -318,6 +392,7 @@
     def stream(columns):
         return pl.BlockSpec((chunk, columns), lambda c: (c, 0))
 
+    indices = pl.BlockSpec((chunk // LANES, 1, LANES), lambda c: (c, 0, 0))
     return pl.pallas_call(
         functools.partial(second_kernel, chunks),
         grid=(chunks,),
@@ -326,7 +401,7 @@
             jax.ShapeDtypeStruct((edges, width), F32),
         ),
         in_specs=[
-            stream(width), stream(width), stream(3), pl.BlockSpec((1, 1, chunk), lambda c: (c, 0, 0)),
+            scalars, stream(width), stream(width), indices, indices,
             whole(table), second(edge_second_weight), whole(edge_gain), whole(edge_offset),
             whole(node_state), second(node_first_weight), whole(node_first_bias), second(node_second_weight),
             whole(node_gain), whole(node_offset),
@@ -334,11 +409,11 @@
         out_specs=(whole(node_state), stream(width)),
         scratch_shapes=[pltpu.VMEM((nodes, width), F32)],
         compiler_params=pltpu.CompilerParams(
-            dimension_semantics=("arbitrary",), vmem_limit_bytes=48 * 2**20
+            dimension_semantics=("arbitrary",), vmem_limit_bytes=67043328
         ),
         name="layer_two",
     )(
-        pre, state, columns, rows, table, edge_second_weight, edge_gain, edge_offset,
+        block_counts, pre, state, senders, receivers, table, edge_second_weight, edge_gain, edge_offset,
         node_state, node_first_weight, node_first_bias, node_second_weight, node_gain, node_offset,
     )
 

time: 63.2 us -> 56.9 us (0.900)
  local copies, waits for them, and re-layouts: 10.4 us -> 3.99 us
  Pallas kernels: 49.9 us -> 51.9 us
  other arithmetic: 1.54 us -> 0 us
    unnamed x24 -> x1, local copies, waits for them, and re-layouts: 8.44 us -> 1.37 us
    reshape x2, local copies, waits for them, and re-layouts: 0.1 us -> 2.62 us  [the longest x1 1.31 us: shards_body(): receivers = edge_receiver.reshape(edges // LANES, 1, LANES)]
    another operation x3 -> x0, local copies, waits for them, and re-layouts: 1.86 us -> none  [shards_body(): jnp.stack([edge_sender, edge_receiver, usable.astype(jnp.int32)], axis=1)]
    pallas_call x1, Pallas kernels: 11.5 us -> 12.7 us  [shards_body(): pl.pallas_call(functools.partial(second_kernel, chunks), grid=(chunks,),...]
    pallas_call x1, Pallas kernels: 38.3 us -> 39.2 us  [shards_body(): pl.pallas_call(functools.partial(first_kernel, patches, bands, chunk), ou...]
    select_n x1 -> x0, other arithmetic: 0.78 us -> none  [shards_body(): rows = jnp.where(usable, edge_receiver, -1).reshape(chunks, 1, chunk)]
    unnamed x1 -> x0, other arithmetic: 0.73 us -> none
where the time goes in v2:
time: 56.9 us; the launch traced here: 56.5 us
  Pallas kernels  51.9 us (91%)
  local copies, waits for them, and re-layouts  3.99 us (7%)
  between operations  0.64 us (1%)
    pallas_call x1, Pallas kernels, shards_body(): pl.pallas_call(functools.partial(first_kernel, patches, bands, chunk), ou...  39.2 us
    pallas_call x1, Pallas kernels, shards_body(): pl.pallas_call(functools.partial(second_kernel, chunks), grid=(chunks,),...  12.7 us
    unnamed x1, local copies, waits for them, and re-layouts  1.37 us
    reshape x1, local copies, waits for them, and re-layouts, shards_body(): receivers = edge_receiver.reshape(edges // LANES, 1, LANES)  1.31 us
    reshape x1, local copies, waits for them, and re-layouts, shards_body(): senders = edge_sender.reshape(edges // LANES, 1, LANES)  1.31 us

profile of v2, /device:TPU:0, one launch (start us, length us, event | category | flops | bytes accessed | tf_op | source)
XLA Modules:
  0.0 56.5 jit_solution(9908432114159835653)
XLA Ops:
  0.6 1.3 %reshape.10.senders_hbm.senders_ref = s32[20,1,128]{2,1,0:T(1,128)} reshape(s32[2560]{0:T(1024)} %param.18) | data formatting | bytes 20480 | tf_op jit(solution)/shard_map/reshape | solution.py:330
  1.9 1.3 %reshape.11.receivers_hbm.receivers_ref = s32[20,1,128]{2,1,0:T(1,128)} reshape(s32[2560]{0:T(1024)} %param.19) | data formatting | bytes 20480 | tf_op jit(solution)/shard_map/reshape | solution.py:331
  3.3 1.4 %copy.18.lists_hbm = s32[1,32,8]{2,1,0:T(8,128)} copy(s32[1,32,8]{1,2,0:T(8,128)} %param.21) | data formatting | bytes 2048 | tf_op args[5]
  4.6 39.2 %layer_one.1 = (f32[320,512]{1,0:T(8,128)}, bf16[256,512]{1,0:T(8,128)(2,1)}, f32[2560,512]{1,0:T(8,128)}, f32[2560,512]{1,0:T(8,128)}) custom-call(s32[20]{0:T(128)} %counts_ref.3, f32[640,256]{1,0:T(8,128)} %lat_hbm.1, s32[20,1,128]{2,1,0:T(1,128)} %reshape.10.senders_hbm.senders_ref, s32[20,1,128]{2,1,0:T(1,128)} %reshape.11.receivers_hbm.receivers_ref, ...), custom_call_target="tpu_custom_call" | custom-call | tf_op jit(solution)/shard_map/layer_one/pallas_call | solution.py:335
  43.8 12.7 %layer_two.1 = (f32[320,512]{1,0:T(8,128)}, f32[2560,512]{1,0:T(8,128)}) custom-call(s32[20]{0:T(128)} %counts_ref.3, f32[2560,512]{1,0:T(8,128)} %get-tuple-element.6.pre_ref, f32[2560,512]{1,0:T(8,128)} %get-tuple-element.7.state_ref, s32[20,1,128]{2,1,0:T(1,128)} %reshape.10.senders_hbm.senders_ref, s32[20,1,128]{2,1,0:T(1,128)} %reshape.11.receivers_hbm.receivers_ref, ...), custom_call_target="tpu_custom_call" | custom-call | tf_op jit(solution)/shard_map/layer_two/pallas_call | solution.py:396
